TPU v7x, 32 devices: a whole 2x2x4 slice. The times are simulated.
32 devices in a mesh: dp: 8 (over y, x, core), fsdp: 4 (over z).
Axes of the slice: x: 2, y: 2, z: 4, core: 2. Of those that a mesh axis runs over, the one named last changes fastest.
Arguments:
- inputs: bfloat16 [32, 8, 12, 6, 6, 256], P(('dp', 'fsdp')), may hold values from -6 to 6
- cotangent: bfloat16 [32, 8, 12, 6, 6, 256], P(('dp', 'fsdp')), may hold values from -6 to 6
- lengths: int32 [32], P(('dp', 'fsdp')), may hold values from 2 to 8
- face_table: int32 [12, 4], replicated, may hold values from 0 to 11
- w_first: float32 [2304, 256], P('fsdp'), may hold values from -0.125 to 0.125
- w_second: float32 [2304, 256], P('fsdp'), may hold values from -0.125 to 0.125
- w_skip: float32 [256, 256], P('fsdp'), may hold values from -0.375 to 0.375
- mom_first: float32 [2304, 256], P('fsdp'), may hold values from -64 to 64
- sq_first: float32 [2304, 256], P('fsdp'), may hold values from 12.16512 to 48.66048
- mom_second: float32 [2304, 256], P('fsdp'), may hold values from -64 to 64
- sq_second: float32 [2304, 256], P('fsdp'), may hold values from 12.16512 to 48.66048
- mom_skip: float32 [256, 256], P('fsdp'), may hold values from -160 to 160
- sq_skip: float32 [256, 256], P('fsdp'), may hold values from 68.56704 to 276.48
Outputs:
- output: bfloat16 [32, 8, 12, 6, 6, 256], P(('dp', 'fsdp'))
- grad_inputs: float32 [32, 8, 12, 6, 6, 256], P(('dp', 'fsdp'))
- new_first: float32 [2304, 256], P('fsdp')
- new_mom_first: float32 [2304, 256], P('fsdp')
- new_sq_first: float32 [2304, 256], P('fsdp')
- new_second: float32 [2304, 256], P('fsdp')
- new_mom_second: float32 [2304, 256], P('fsdp')
- new_sq_second: float32 [2304, 256], P('fsdp')
- new_skip: float32 [256, 256], P('fsdp')
- new_mom_skip: float32 [256, 256], P('fsdp')
- new_sq_skip: float32 [256, 256], P('fsdp')
All inputs are finite; a program needn't handle non-finite values.
Results may differ from a plain program's by a relative error of at most 0.019.
Values may be sent and summed in bfloat16 or wider, within the bound.
No kernel may reach another device: no remote copies, remote signals or barrier semaphores. Data moves between devices by JAX's collectives and lax.ppermute only.
A program may use at most 256 MiB of HBM per device.

v0:
```python
import jax
import jax.numpy as jnp
from jax import lax
from jax.sharding import PartitionSpec as P

C = 256
STEP_COUNT = 10
tap_offsets = [(row_off, col_off) for row_off in range(3) for col_off in range(3)]


def face_hots(face_table, dtype):
    faces = face_table.shape[0]
    labels = jnp.arange(faces, dtype=jnp.int32)
    return [
        (face_table[:, corner_side][:, None] == labels[None, :]).astype(dtype)
        for corner_side in range(4)
    ]


def pad_faces(field, hots):

    def route(matrix, edge, form):
        return jnp.einsum(form, matrix, edge, preferred_element_type=jnp.float32).astype(
            jnp.bfloat16
        )

    north = route(hots[0], field[:, :, -1], "fh,rhwc->rfwc")
    east = route(hots[1], field[:, :, :, 0], "fh,rhwc->rfwc")
    south = route(hots[2], field[:, :, 0], "fh,rhwc->rfwc")
    west = route(hots[3], field[:, :, :, -1], "fh,rhwc->rfwc")
    middle = jnp.concatenate([west[:, :, :, None], field, east[:, :, :, None]], axis=3)
    top_row = jnp.pad(north, ((0, 0), (0, 0), (1, 1), (0, 0)))
    bottom_row = jnp.pad(south, ((0, 0), (0, 0), (1, 1), (0, 0)))
    return jnp.concatenate([top_row[:, :, None], middle, bottom_row[:, :, None]], axis=2)


def unpad_back(spread, hots):
    highest = lax.Precision.HIGHEST
    inner = spread[:, :, 1:-1, 1:-1]
    inner = inner.at[:, :, -1].add(
        jnp.einsum("fh,rfwc->rhwc", hots[0], spread[:, :, 0, 1:-1], precision=highest)
    )
    inner = inner.at[:, :, :, 0].add(
        jnp.einsum("fh,rfwc->rhwc", hots[1], spread[:, :, 1:-1, -1], precision=highest)
    )
    inner = inner.at[:, :, 0].add(
        jnp.einsum("fh,rfwc->rhwc", hots[2], spread[:, :, -1, 1:-1], precision=highest)
    )
    inner = inner.at[:, :, :, -1].add(
        jnp.einsum("fh,rfwc->rhwc", hots[3], spread[:, :, 1:-1, 0], precision=highest)
    )
    return inner


def conv_apply(padded, weight):
    edge_len = padded.shape[2] - 2
    channels = weight.shape[1]
    taps_weight = weight.reshape(9, channels, channels)
    flat_padded = padded.reshape(-1, channels)
    products = jnp.einsum(
        "pc,tcd->ptd", flat_padded, taps_weight, preferred_element_type=jnp.float32
    )
    products = products.reshape(padded.shape[:4] + (9, channels))
    summed = None
    for tap_index, (row_off, col_off) in enumerate(tap_offsets):
        part = products[:, :, row_off : row_off + edge_len, col_off : col_off + edge_len, tap_index]
        summed = part if summed is None else summed + part
    return summed


def conv_back(padded, grad, weight):
    channels = weight.shape[1]
    taps_weight = weight.reshape(9, channels, channels)
    flat_grad = grad.reshape(-1, channels)
    pulled = jnp.einsum("pd,tcd->ptc", flat_grad, taps_weight, preferred_element_type=jnp.float32)
    pulled = pulled.reshape(grad.shape[:4] + (9, channels))
    spread = None
    placed = []
    for tap_index, (row_off, col_off) in enumerate(tap_offsets):
        widths = ((0, 0), (0, 0), (row_off, 2 - row_off), (col_off, 2 - col_off), (0, 0))
        moved = jnp.pad(pulled[:, :, :, :, tap_index], widths)
        spread = moved if spread is None else spread + moved
        placed.append(jnp.pad(grad, widths))
    stacked = jnp.stack(placed, axis=4).reshape(-1, 9, channels)
    flat_padded = padded.reshape(-1, channels)
    weight_grad = jnp.einsum(
        "pc,ptd->tcd", flat_padded, stacked, preferred_element_type=jnp.float32
    )
    return (weight_grad.reshape(9 * channels, channels), spread)


def gelu_tanh(v):
    return jax.nn.gelu(v, approximate=True)


def forward_pass(fields, hots_low, gathered):
    pad_in = pad_faces(fields, hots_low)
    pre_one = conv_apply(pad_in, gathered[0])
    hidden = gelu_tanh(pre_one).astype(jnp.bfloat16)
    pad_hidden = pad_faces(hidden, hots_low)
    pre_two = conv_apply(pad_hidden, gathered[1])
    return (pad_in, pre_one, pad_hidden, pre_two)


def adamw(weight, moment, square, grad, rate):
    moment_new = 0.9 * moment + 0.1 * grad
    square_new = 0.999 * square + 0.001 * grad * grad
    fix_one = 1.0 - 0.9**STEP_COUNT
    fix_two = 1.0 - 0.999**STEP_COUNT
    weight_new = weight - rate * (
        moment_new / fix_one / (jnp.sqrt(square_new / fix_two) + 1e-08) + 0.01 * weight
    )
    return (weight_new, moment_new, square_new)


def per_device(
    inputs,
    cotangent,
    lengths,
    face_table,
    w_first,
    w_second,
    w_skip,
    mom_first,
    sq_first,
    mom_second,
    sq_second,
    mom_skip,
    sq_skip,
):
    fields = inputs[0]
    channels = fields.shape[-1]
    hots_low = face_hots(face_table, jnp.bfloat16)
    hots_full = face_hots(face_table, jnp.float32)
    low_weights = (
        w_first.astype(jnp.bfloat16),
        w_second.astype(jnp.bfloat16),
        w_skip.astype(jnp.bfloat16),
    )
    gathered = (
        lax.all_gather(low_weights[0], "fsdp", axis=0, tiled=True),
        lax.all_gather(low_weights[1], "fsdp", axis=0, tiled=True),
        lax.all_gather(low_weights[2], "fsdp", axis=0, tiled=True),
    )
    saved = forward_pass(fields, hots_low, gathered)
    flat_fields = fields.reshape(-1, channels)
    skipped = jnp.dot(flat_fields, gathered[2], preferred_element_type=jnp.float32).reshape(
        fields.shape
    )
    output = (gelu_tanh(saved[3]) + skipped).astype(jnp.bfloat16)
    gathered = (
        lax.all_gather(low_weights[0], "fsdp", axis=0, tiled=True),
        lax.all_gather(low_weights[1], "fsdp", axis=0, tiled=True),
        lax.all_gather(low_weights[2], "fsdp", axis=0, tiled=True),
    )
    saved = forward_pass(fields, hots_low, gathered)
    pad_in, pre_one, pad_hidden, pre_two = saved
    live = (jnp.arange(fields.shape[0]) < lengths[0]).astype(jnp.bfloat16)
    grad_out = cotangent[0] * live[:, None, None, None, None]
    flat_out = grad_out.reshape(-1, channels)
    dw_skip = lax.dot_general(
        flat_fields, flat_out, (((0,), (0,)), ((), ())), preferred_element_type=jnp.float32
    )
    gelu_pull_two = jax.vjp(gelu_tanh, pre_two)[1]
    grad_two = gelu_pull_two(grad_out.astype(jnp.float32))[0].astype(jnp.bfloat16)
    dw_second, spread_hidden = conv_back(pad_hidden, grad_two, gathered[1])
    grad_hidden = unpad_back(spread_hidden, hots_full)
    gelu_pull_one = jax.vjp(gelu_tanh, pre_one)[1]
    grad_one = gelu_pull_one(grad_hidden)[0].astype(jnp.bfloat16)
    dw_first, spread_in = conv_back(pad_in, grad_one, gathered[0])
    skip_back = lax.dot_general(
        flat_out, gathered[2], (((1,), (1,)), ((), ())), preferred_element_type=jnp.float32
    )
    grad_inputs = unpad_back(spread_in, hots_full) + skip_back.reshape(fields.shape)
    shards = (
        lax.psum_scatter(
            dw_first.astype(jnp.bfloat16), "fsdp", scatter_dimension=0, tiled=True
        ).astype(jnp.float32),
        lax.psum_scatter(
            dw_second.astype(jnp.bfloat16), "fsdp", scatter_dimension=0, tiled=True
        ).astype(jnp.float32),
        lax.psum_scatter(
            dw_skip.astype(jnp.bfloat16), "fsdp", scatter_dimension=0, tiled=True
        ).astype(jnp.float32),
    )
    rate_conv = (9 * C) ** (-0.5)
    rate_skip = C ** (-0.5)
    totals = (
        lax.psum(shards[0].astype(jnp.bfloat16), "dp").astype(jnp.float32),
        lax.psum(shards[1].astype(jnp.bfloat16), "dp").astype(jnp.float32),
        lax.psum(shards[2].astype(jnp.bfloat16), "dp").astype(jnp.float32),
    )
    first_set = adamw(w_first, mom_first, sq_first, totals[0], rate_conv)
    second_set = adamw(w_second, mom_second, sq_second, totals[1], rate_conv)
    skip_set = adamw(w_skip, mom_skip, sq_skip, totals[2], rate_skip)
    return (
        output[None],
        grad_inputs[None],
        first_set[0],
        first_set[1],
        first_set[2],
        second_set[0],
        second_set[1],
        second_set[2],
        skip_set[0],
        skip_set[1],
        skip_set[2],
    )


def solution(mesh):
    placed = (
        P(("dp", "fsdp"), None, None, None, None, None),
        P(("dp", "fsdp"), None, None, None, None, None),
        P(("dp", "fsdp")),
        P(),
        P("fsdp", None),
        P("fsdp", None),
        P("fsdp", None),
        P("fsdp", None),
        P("fsdp", None),
        P("fsdp", None),
        P("fsdp", None),
        P("fsdp", None),
        P("fsdp", None),
    )
    return jax.shard_map(
        per_device,
        mesh=mesh,
        in_specs=placed,
        out_specs=(
            P(("dp", "fsdp"), None, None, None, None, None),
            P(("dp", "fsdp"), None, None, None, None, None),
            P("fsdp", None),
            P("fsdp", None),
            P("fsdp", None),
            P("fsdp", None),
            P("fsdp", None),
            P("fsdp", None),
            P("fsdp", None),
            P("fsdp", None),
            P("fsdp", None),
        ),
        check_vma=False,
    )
```

profile of v0, /device:TPU:0, one launch (start us, length us, event | category | flops | bytes accessed | tf_op | source)
XLA Modules:
  0.0 511.8 jit_solution(13693216425621798046)
XLA Ops:
  7.9 5.0 fusion.84
  12.9 0.8 copy.411
  15.4 2.5 copy.510
  18.0 2.2 fusion.39
  22.2 2.4 maximum_bitcast_fusion
  24.7 11.0 %reduce-scatter.10.cloned.1.call-done = bf16[64,256]{1,0:T(8,128)(2,1)} async-done(((bf16[256,256]{1,0:T(8,128)(2,1)}), bf16[64,256]{1,0:T(8,128)(2,1)}) %reduce-scatter.10.cloned.1.call-update) | async-done | bytes 32784 | tf_op jit(solution)/shard_map/reduce_scatter | solution.py:182
  35.7 23.7 %psum.23 = bf16[64,256]{1,0:T(8,128)(2,1)S(1)} all-reduce(bf16[64,256]{1,0:T(8,128)(2,1)} %reduce-scatter.10.cloned.1.call-done), channel_id=1, replica_groups=mesh['dp'=8,'fsdp'=4] {'dp'}, use_global_device_ids=true, to_apply=%region_5.6 | all-reduce | flops 16384 | bytes 65536 | tf_op jit(solution)/shard_map/psum | solution.py:191
  60.2 14.7 %all_gather.14 = bf16[256,256]{1,0:T(8,128)(2,1)} all-gather(bf16[64,256]{1,0:T(8,128)(2,1)S(1)} %get-tuple-element.194), channel_id=1, replica_groups=mesh['dp'=8,'fsdp'=4] {'fsdp'}, dimensions={0}, use_global_device_ids=true | all-gather | bytes 163840 | tf_op jit(solution)/shard_map/all_gather | solution.py:143
  74.8 24.0 %fusion.33 = f32[8,12,8,8,9,256]{5,3,4,2,1,0:T(8,128)} fusion(bf16[9,256,256,1,1,1]{2,1,0,5,4,3:T(8,128)(2,1)} %bitcast.404, bf16[8,12,8,8,256,1]{4,1,3,0,2,5:T(8,128)(2,1)} %maximum_bitcast_fusion), kind=kOutput, calls=%fused_computation.102 | convolution fusion | flops 7247757312 | bytes 60948480 | tf_op jit(solution)/shard_map/pc,tcd->ptd/dot_general | solution.py:60
  98.8 17.8 %multiply_convert_fusion = (bf16[8,12,6,6,256]{4,3,2,1,0:T(8,128)(2,1)S(1)}, f32[8,12,6,6,256]{4,3,2,1,0:T(8,128)}) fusion(f32[8,12,8,8,9,256]{5,3,4,2,1,0:T(8,128)} %fusion.33), kind=kLoop, calls=%fused_computation.78 | loop fusion | flops 15040512 | bytes 37158912 | tf_op jit(solution)/shard_map/convert_element_type | solution.py:99
  117.2 1.1 copy.300
  118.8 1.0 copy.301
  119.8 0.8 fusion.176
  122.3 0.8 copy-done.15
  123.0 22.2 %fusion.115 = f32[8,12,8,8,9,256]{5,3,2,1,0,4:T(8,128)} fusion(bf16[9,256,256,1,1,1]{2,1,5,4,3,0:T(8,128)(2,1)} %bitcast.402, bf16[8,12,1,8,256]{4,3,2,1,0:T(8,128)(2,1)} %copy.301, bf16[8,12,6,1,256]{4,3,2,1,0:T(2,128)(2,1)S(1)} %copy.296, bf16[8,12,6,6,256]{4,3,2,1,0:T(8,128)(2,1)S(1)} %get-tuple-element.164, bf16[8,12,6,1,256]{4,3,2,1,0:T(2,128)(2,1)S(1)} %copy.295, ...), kind=kOutput, calls=%fused_computation.210 | convolution fusion | flops 7263485952 | bytes 60948480 | tf_op jit(solution)/shard_map/pc,tcd->ptd/dot_general | solution.py:60
  145.3 18.2 %fusion.7 = (bf16[8,12,6,6,256]{4,3,2,1,0:T(8,128)(2,1)S(1)}, f32[8,12,6,6,1,256]{5,3,2,1,0,4:T(8,128)}) fusion(bf16[8]{0:T(256)(128)(2,1)S(1)} %copy-done.29, bf16[1,8,12,6,6,256]{5,1,4,3,2,0:T(8,128)(2,1)S(1)} %copy-done.1, f32[8,12,8,8,9,256]{5,3,2,1,0,4:T(8,128)} %fusion.115), kind=kLoop, calls=%fused_computation.19 | loop fusion | flops 26542080 | bytes 38928400 | tf_op jit(solution)/shard_map/convert_element_type | solution.py:165
  163.5 19.7 %fusion.40 = f32[8,12,6,6,9,256]{5,3,2,1,0,4:T(8,128)} fusion(bf16[9,256,256,1,1,1]{2,1,5,4,3,0:T(8,128)(2,1)S(1)} %bitcast.403, f32[8,12,6,6,1,256]{5,3,2,1,0,4:T(8,128)} %get-tuple-element.163, bf16[1,8,12,6,6,256]{5,1,4,3,2,0:T(8,128)(2,1)} %param.30, bf16[8]{0:T(256)(128)(2,1)} %copy-done.28), kind=kOutput, calls=%fused_computation.113 | convolution fusion | flops 4098097152 | bytes 38338576 | tf_op jit(solution)/shard_map/pd,tcd->ptc/dot_general | solution.py:75
  183.2 30.6 %slice_bitcast_fusion.17 = (f32[8,12,6,6,256]{4,3,2,1,0:T(8,128)}, f32[8,12,6,6,256]{4,3,2,1,0:T(8,128)}, f32[8,12,6,6,256]{4,3,2,1,0:T(8,128)}, f32[8,12,6,6,25...) fusion(f32[8,12,6,6,9,256]{5,3,2,1,0,4:T(8,128)} %fusion.40), kind=kLoop, calls=%fused_computation.56 | loop fusion | bytes 63700992 | tf_op jit(solution)/shard_map/squeeze | solution.py:81
  213.8 18.5 %pad_add_fusion.1 = f32[8,12,8,8,256]{4,3,2,1,0:T(8,128)} fusion(f32[8,12,6,6,256]{4,3,2,1,0:T(8,128)} %get-tuple-element.183, f32[8,12,6,6,256]{4,3,2,1,0:T(8,128)} %get-tuple-element.176, f32[8,12,6,6,256]{4,3,2,1,0:T(8,128)} %get-tuple-element.177, f32[8,12,6,6,256]{4,3,2,1,0:T(8,128)} %get-tuple-element.178, f32[8,12,6,6,256]{4,3,2,1,0:T(8,128)} %get-tuple-element.179, ...), kind=kLoop, calls=%fused_computation.7 | loop fusion | flops 12582912 | bytes 38141952 | tf_op jit(solution)/shard_map/add | solution.py:82
  232.3 4.9 fusion.175
  237.2 2.7 slice_bitcast_fusion.26
  239.9 5.3 %slice.563 = f32[8,12,6,6,256]{4,3,2,1,0:T(8,128)} slice(f32[8,12,8,8,256]{4,3,2,1,0:T(8,128)} %pad_add_fusion.1), slice={[0:8], [0:12], [1:7], [1:7], [0:256]} | slice | bytes 7077888 | tf_op jit(solution)/shard_map/slice | solution.py:39
  245.2 2.3 bitcast_dynamic-update-slice_fusion.8
  247.5 2.5 bitcast_dynamic-update-slice_fusion.7
  249.9 2.5 bitcast_dynamic-update-slice_fusion.6
  252.4 2.4 bitcast_dynamic-update-slice_fusion.5
  254.8 2.4 bitcast_dynamic-update-slice_fusion.4
  257.2 2.4 bitcast_dynamic-update-slice_fusion.3
  259.7 2.4 bitcast_dynamic-update-slice_fusion.2
  262.1 2.5 bitcast_dynamic-update-slice_fusion.1
  264.5 2.4 bitcast_dynamic-update-slice_fusion
  267.0 13.9 %bitcast_convert_fusion = bf16[9,256,256]{1,2,0:T(8,128)(2,1)} fusion(bf16[8,12,8,8,9,256]{5,3,2,1,0,4:T(8,128)(2,1)} %bitcast_dynamic-update-slice_fusion, bf16[8,12,1,8,256]{4,3,2,1,0:T(8,128)(2,1)S(1)} %copy-done.19, bf16[8,12,6,1,256]{4,3,2,1,0:T(2,128)(2,1)S(1)} %copy-done.16, bf16[8,12,6,6,256]{4,3,2,1,0:T(8,128)(2,1)S(1)} %copy-done.3, ...), kind=kOutput, calls=%fused_computation.111 | convolution fusion | flops 7264075776 | bytes 32636928 | tf_op jit(solution)/shard_map/pc,ptd->tcd/dot_general | solution.py:86
  283.8 2.6 fusion.90
  286.4 3.2 slice_add_fusion.19
  289.6 13.0 %scatter-add.29 = f32[8,12,6,6,256]{4,3,2,1,0:T(8,128)} dynamic-update-slice(f32[8,12,6,6,256]{4,3,2,1,0:T(8,128)} %fusion.90, f32[8,12,6,1,256]{4,3,2,1,0:T(1,128)S(1)} %slice_add_fusion.19, s32[]{:T(128)} %constant.226.clone.1, s32[]{:T(128)} %constant.226.clone.1, s32[]{:T(128)} %constant.226.clone.1, s32[]{:T(128)} %constant.226.clone.1, s32[]{:T(128)} %constant.226.clone.1) | dynamic-update-slice | bytes 1179652 | tf_op jit(solution)/shard_map/scatter-add | solution.py:43
  302.6 2.5 fusion.89
  305.1 3.4 slice_add_fusion.18
  308.5 13.0 %scatter-add.31 = f32[8,12,6,6,256]{4,3,2,1,0:T(8,128)} dynamic-update-slice(f32[8,12,6,6,256]{4,3,2,1,0:T(8,128)} %fusion.89, f32[8,12,6,1,256]{4,3,2,1,0:T(1,128)S(1)} %slice_add_fusion.18, s32[]{:T(128)} %constant.226.clone.1, s32[]{:T(128)} %constant.226.clone.1, s32[]{:T(128)} %constant.226.clone.1, s32[]{:T(128)} %constant.227.clone.1, s32[]{:T(128)} %constant.226.clone.1) | dynamic-update-slice | bytes 1179652 | tf_op jit(solution)/shard_map/scatter-add | solution.py:49
  321.5 5.5 %fusion.16 = bf16[8,12,6,6,256]{4,3,2,1,0:T(8,128)(2,1)S(1)} fusion(f32[8,12,6,6,256]{4,3,2,1,0:T(8,128)} %get-tuple-element.165, f32[8,12,6,6,256]{4,3,2,1,0:T(8,128)} %scatter-add.31), kind=kLoop, calls=%fused_computation.28 | loop fusion | flops 17694720 | bytes 8847360 | tf_op jit(solution)/shard_map/convert_element_type | solution.py:169
  327.0 2.3 bitcast_dynamic-update-slice_fusion.17
  329.3 2.4 bitcast_dynamic-update-slice_fusion.16
  331.8 2.4 bitcast_dynamic-update-slice_fusion.15
  334.2 2.3 bitcast_dynamic-update-slice_fusion.14
  336.5 2.4 bitcast_dynamic-update-slice_fusion.13
  338.9 2.4 bitcast_dynamic-update-slice_fusion.12
  341.4 2.4 bitcast_dynamic-update-slice_fusion.11
  343.8 2.4 bitcast_dynamic-update-slice_fusion.10
  346.2 2.5 bitcast_dynamic-update-slice_fusion.9
  348.7 16.7 %fusion.43 = f32[8,12,6,6,9,256]{5,1,4,3,2,0:T(8,128)} fusion(bf16[9,256,256,1,1,1]{2,1,0,5,4,3:T(8,128)(2,1)S(1)} %bitcast.405, bf16[8,12,6,6,256,1]{4,3,2,1,0,5:T(8,128)(2,1)S(1)} %bitcast.397), kind=kOutput, calls=%fused_computation.116 | convolution fusion | flops 4076863488 | bytes 34799616 | tf_op jit(solution)/shard_map/pd,tcd->ptc/dot_general | solution.py:75
  365.3 31.7 %slice_bitcast_fusion.8 = (f32[8,12,6,6,256]{4,1,3,2,0:T(8,128)}, f32[8,12,6,6,256]{4,1,3,2,0:T(8,128)}, f32[8,12,6,6,256]{4,1,3,2,0:T(8,128)}, f32[8,12,6,6,256...) fusion(f32[8,12,6,6,9,256]{5,1,4,3,2,0:T(8,128)} %fusion.43), kind=kLoop, calls=%fused_computation.47 | loop fusion | bytes 63700992 | tf_op jit(solution)/shard_map/squeeze | solution.py:81
  397.0 15.3 %bitcast_convert_fusion.1 = bf16[9,256,256]{1,2,0:T(8,128)(2,1)} fusion(bf16[8,12,8,8,9,256]{5,3,2,1,0,4:T(8,128)(2,1)} %bitcast_dynamic-update-slice_fusion.9, bf16[8,12,8,8,256,1]{4,1,3,0,2,5:T(8,128)(2,1)} %maximum_bitcast_fusion), kind=kOutput, calls=%fused_computation.112 | convolution fusion | flops 7248347136 | bytes 32636928 | tf_op jit(solution)/shard_map/pc,ptd->tcd/dot_general | solution.py:86
  412.4 4.9 fusion.53
  417.3 3.1 copy.352
  420.4 14.8 %pad_add_fusion = f32[8,12,8,8,256]{4,1,3,2,0:T(8,128)S(1)} fusion(f32[8,12,6,6,256]{4,1,3,2,0:T(8,128)} %get-tuple-element.173, f32[8,12,6,6,256]{4,1,3,2,0:T(8,128)} %get-tuple-element.174, f32[8,12,6,6,256]{4,1,3,2,0:T(8,128)} %get-tuple-element.167, f32[8,12,6,6,256]{4,1,3,2,0:T(8,128)} %get-tuple-element.168, f32[8,12,6,6,256]{4,1,3,2,0:T(8,128)} %get-tuple-element.169, ...), kind=kLoop, calls=%fused_computation | loop fusion | flops 12582912 | bytes 38141952 | tf_op jit(solution)/shard_map/add | solution.py:82
  435.3 2.7 slice.581
  438.0 1.4 fusion.61
  439.4 2.6 fusion.63
  442.0 2.5 fusion.65
  444.5 2.5 fusion.67
  447.1 3.3 add_bitcast_fusion
  450.4 3.8 copy.353
  454.3 45.6 %all-reduce.43.cloned.1.call-done = (bf16[576,256]{1,0:T(8,128)(2,1)}, bf16[576,256]{1,0:T(8,128)(2,1)}) async-done(((bf16[576,256]{1,0:T(8,128)(2,1)}, bf16[576,256]{1,0:T(8,128)(2,1)}), (bf16[576,256]{1,0:T(8,128)(2,1)}, bf16[576,256]{1,0:T(8,128)(2,1)})) %all-reduce.43.cloned.1.call-update) | async-done | bytes 589840 | tf_op jit(solution)/shard_map/psum | solution.py:189
  499.8 2.4 multiply_subtract_fusion.1
  502.3 2.4 multiply_subtract_fusion
  (107 shorter events, 10.1 us)
Async XLA Ops:
  7.2 28.6 %reduce-scatter.10.cloned.1.call-start = ((), (), s32[]{:S(2)}) async-start(), calls=%async_computation.7 | async-start | bytes 163840 | tf_op jit(solution)/shard_map/reduce_scatter | solution.py:182
  7.9 10.1 %copy-start.28 = (bf16[8]{0:T(256)(128)(2,1)}, bf16[8]{0:T(256)(128)(2,1)S(1)}, u32[]{:S(2)}) copy-start(bf16[8]{0:T(256)(128)(2,1)S(1)} %compare_convert_fusion) | copy-start | bytes 52
  7.9 5.9 %copy-start.9 = (f32[576,256]{1,0:T(8,128)S(1)}, f32[576,256]{1,0:T(8,128)}, u32[]{:S(2)}) copy-start(f32[576,256]{1,0:T(8,128)} %param.33) | copy-start | bytes 1769476
  7.9 6.7 %copy-start.11 = (f32[576,256]{1,0:T(8,128)S(1)}, f32[576,256]{1,0:T(8,128)}, u32[]{:S(2)}) copy-start(f32[576,256]{1,0:T(8,128)} %param.34) | copy-start | bytes 1769476
  12.9 5.1 copy-start
  13.7 61.1 %all-gather.3.cloned.1.call-start = ((), (), s32[]{:S(2)}) async-start(), calls=%async_computation.3 | async-start | bytes 1474560 | tf_op jit(solution)/shard_map/all_gather | solution.py:141
  14.5 5.6 %copy-start.30 = (s32[12,4]{0,1:T(4,128)S(1)}, s32[12,4]{0,1:T(4,128)}, u32[]{:S(2)}) copy-start(s32[12,4]{0,1:T(4,128)} %param.32) | copy-start | bytes 580
  14.5 107.7 %all-gather.5.cloned.1.call-start = ((), (), s32[]{:S(2)}) async-start(), calls=%async_computation.4 | async-start | bytes 1474560 | tf_op jit(solution)/shard_map/all_gather | solution.py:142
  15.4 431.7 %reduce-scatter.8.cloned.1.call-start = ((), (), s32[]{:S(2)}) async-start(), calls=%async_computation.6 | async-start | bytes 1474560 | tf_op jit(solution)/shard_map/reduce_scatter | solution.py:179
  22.1 37.4 %copy-start.25 = (f32[64,256]{1,0:T(8,128)S(1)}, f32[64,256]{1,0:T(8,128)}, u32[]{:S(2)}) copy-start(f32[64,256]{1,0:T(8,128)} %param.35) | copy-start | bytes 196612
  22.1 37.4 %copy-start.26 = (f32[64,256]{1,0:T(8,128)S(1)}, f32[64,256]{1,0:T(8,128)}, u32[]{:S(2)}) copy-start(f32[64,256]{1,0:T(8,128)} %param.40) | copy-start | bytes 196612
  22.1 37.4 %copy-start.27 = (f32[64,256]{1,0:T(8,128)S(1)}, f32[64,256]{1,0:T(8,128)}, u32[]{:S(2)}) copy-start(f32[64,256]{1,0:T(8,128)} %param.41) | copy-start | bytes 196612
  116.6 5.7 %copy-start.2 = (bf16[8,12,6,6,256]{4,3,2,1,0:T(8,128)(2,1)}, bf16[8,12,6,6,256]{4,3,2,1,0:T(8,128)(2,1)S(1)}, u32[]{:S(2)}) copy-start(bf16[8,12,6,6,256]{4,3,2,1,0:T(8,128)(2,1)S(1)} %get-tuple-element.164) | copy-start | bytes 5308420
  121.4 0.9 copy-start.13
  122.2 0.8 copy-start.15
  123.0 22.3 %copy-start.1 = (bf16[1,8,12,6,6,256]{5,1,4,3,2,0:T(8,128)(2,1)S(1)}, bf16[1,8,12,6,6,256]{5,1,4,3,2,0:T(8,128)(2,1)}, u32[]{:S(2)}) copy-start(bf16[1,8,12,6,6,256]{5,1,4,3,2,0:T(8,128)(2,1)} %param.30) | copy-start | bytes 5308420
  123.0 22.3 %copy-start.29 = (bf16[8]{0:T(256)(128)(2,1)S(1)}, bf16[8]{0:T(256)(128)(2,1)}, u32[]{:S(2)}) copy-start(bf16[8]{0:T(256)(128)(2,1)} %copy-done.28) | copy-start | bytes 52
  145.3 18.2 %copy-start.5 = (bf16[2304,256]{1,0:T(8,128)(2,1)S(1)}, bf16[2304,256]{1,0:T(8,128)(2,1)}, u32[]{:S(2)}) copy-start(bf16[2304,256]{1,0:T(8,128)(2,1)} %all-gather.5.cloned.1.call-done) | copy-start | bytes 3538948
  262.0 4.9 copy-start.3
  262.0 4.9 copy-start.14
  262.0 4.9 copy-start.16
  262.0 4.9 copy-start.18
  262.0 4.9 copy-start.19
  280.9 1.5 copy-start.8
  280.9 2.2 copy-start.7
  280.9 166.2 %reduce-scatter.6.cloned.1.call-start = ((), (), s32[]{:S(2)}) async-start(), calls=%async_computation.5 | async-start | bytes 1474560 | tf_op jit(solution)/shard_map/reduce_scatter | solution.py:176
  343.8 4.9 copy-start.6
  397.0 15.4 %copy-start.17 = (bf16[1,8,12,6,6,256]{5,1,4,3,2,0:T(8,128)(2,1)S(1)}, bf16[1,8,12,6,6,256]{5,1,4,3,2,0:T(8,128)(2,1)}, u32[]{:S(2)}) copy-start(bf16[1,8,12,6,6,256]{5,1,4,3,2,0:T(8,128)(2,1)} %param.29) | copy-start | bytes 5308420
  397.0 15.4 %copy-start.24 = (bf16[256,256]{1,0:T(8,128)(2,1)S(1)}, bf16[256,256]{1,0:T(8,128)(2,1)}, u32[]{:S(2)}) copy-start(bf16[256,256]{1,0:T(8,128)(2,1)} %all_gather.14) | copy-start | bytes 393220
  412.4 87.5 %all-reduce.43.cloned.1.call-start = ((), (), s32[]{:S(2)}) async-start(), calls=%async_computation.8 | async-start | bytes 1179648 | tf_op jit(solution)/shard_map/psum | solution.py:189
  438.0 9.1 %copy-start.4 = (bf16[8,12,6,6,256]{4,3,2,1,0:T(8,128)(2,1)S(1)}, bf16[8,12,6,6,256]{4,3,2,1,0:T(8,128)(2,1)}, u32[]{:S(2)}) copy-start(bf16[8,12,6,6,256]{4,3,2,1,0:T(8,128)(2,1)} %fusion.39) | copy-start | bytes 5308420
  450.4 49.5 %copy-start.10 = (f32[576,256]{1,0:T(8,128)S(1)}, f32[576,256]{1,0:T(8,128)}, u32[]{:S(2)}) copy-start(f32[576,256]{1,0:T(8,128)} %param.33) | copy-start | bytes 1769476
  450.4 49.5 %copy-start.20 = (f32[576,256]{1,0:T(8,128)S(1)}, f32[576,256]{1,0:T(8,128)}, u32[]{:S(2)}) copy-start(f32[576,256]{1,0:T(8,128)} %param.36) | copy-start | bytes 1769476
  450.4 49.5 %copy-start.21 = (f32[576,256]{1,0:T(8,128)S(1)}, f32[576,256]{1,0:T(8,128)}, u32[]{:S(2)}) copy-start(f32[576,256]{1,0:T(8,128)} %param.37) | copy-start | bytes 1769476
  450.4 51.9 %copy-start.12 = (f32[576,256]{1,0:T(8,128)S(1)}, f32[576,256]{1,0:T(8,128)}, u32[]{:S(2)}) copy-start(f32[576,256]{1,0:T(8,128)} %param.34) | copy-start | bytes 1769476
  450.4 51.9 %copy-start.22 = (f32[576,256]{1,0:T(8,128)S(1)}, f32[576,256]{1,0:T(8,128)}, u32[]{:S(2)}) copy-start(f32[576,256]{1,0:T(8,128)} %param.38) | copy-start | bytes 1769476
  450.4 51.9 %copy-start.23 = (f32[576,256]{1,0:T(8,128)S(1)}, f32[576,256]{1,0:T(8,128)}, u32[]{:S(2)}) copy-start(f32[576,256]{1,0:T(8,128)} %param.39) | copy-start | bytes 1769476
Sparse Core Ops, SparseCore 0:
  13.8 21.8 reduce-scatter.9
  38.0 30.0 all-gather.2
  70.2 29.5 all-gather.4
  281.0 26.5 reduce-scatter.7
  412.5 26.7 reduce-scatter.5
  447.2 52.5 all-reduce.42
where the time goes:
time: 519 us; the launch traced here: 512 us
  local copies, waits for them, and re-layouts  163 us (31%)
  matrix products  139 us (27%)
  other arithmetic  98.3 us (19%)
  waiting for transfers between devices  56.7 us (11%)
  blocking collectives  38.4 us (7%)
  between operations  15.6 us (3%)
    squeeze x2, local copies, waits for them, and re-layouts, conv_back(): moved = jnp.pad(pulled[:, :, :, :, tap_index], widths)  62.2 us
    unnamed x82, local copies, waits for them, and re-layouts  49.7 us
    dot_general x2, matrix products, conv_apply(): jnp.einsum('pc,tcd->ptd', flat_padded, taps_weight, preferred_element_typ...  46.2 us
    psum x1, waiting for transfers between devices, per_device(): lax.psum(shards[0].astype(jnp.bfloat16), 'dp').astype(jnp.float32)  45.6 us
    dot_general x2, matrix products, conv_back(): jnp.einsum('pd,tcd->ptc', flat_grad, taps_weight, preferred_element_type=...  36.3 us
    add x2, other arithmetic, conv_back(): spread = moved if spread is None else spread + moved  33.3 us
    dot_general x2, matrix products, conv_back(): jnp.einsum('pc,ptd->tcd', flat_padded, stacked, preferred_element_type=jn...  29.2 us
    psum x1, blocking collectives, per_device(): lax.psum(shards[2].astype(jnp.bfloat16), 'dp').astype(jnp.float32)  23.7 us
  transfers between devices with their start and end apart: 6, of which 2 were waited for; matrix products, arithmetic and copies ran while one was open for 45% of the time, Pallas kernels for 0%

commit v1 on v0

--- a/solution.py
+++ b/solution.py
@@ -6,6 +6,28 @@
 C = 256
 STEP_COUNT = 10
 tap_offsets = [(row_off, col_off) for row_off in range(3) for col_off in range(3)]
+
+
+def laid_out(pieces, dim):
+    pieces = jnp.moveaxis(pieces, 0, dim)
+    dims = pieces.shape
+    return pieces.reshape(*dims[:dim], dims[dim] * dims[dim + 1], *dims[dim + 2 :])
+
+
+def doubled(x, axis):
+    length = lax.axis_size(axis)
+    parts = x[None]
+    for level in range(length.bit_length() - 1):
+        bit = 1 << level
+        partner_block = lax.ppermute(parts, axis, [(i, i ^ bit) for i in range(length)])
+        both = jnp.stack([parts, partner_block])
+        upper = lax.axis_index(axis) >> level & 1
+        parts = jnp.where(upper == 0, both, both[::-1]).reshape(-1, *x.shape)
+    return parts
+
+
+def collect(value, axis, dim):
+    return laid_out(doubled(value, axis), dim)
 
 
 def face_hots(face_table, dtype):
@@ -140,7 +162,7 @@
     gathered = (
         lax.all_gather(low_weights[0], "fsdp", axis=0, tiled=True),
         lax.all_gather(low_weights[1], "fsdp", axis=0, tiled=True),
-        lax.all_gather(low_weights[2], "fsdp", axis=0, tiled=True),
+        collect(low_weights[2], "fsdp", 0),
     )
     saved = forward_pass(fields, hots_low, gathered)
     flat_fields = fields.reshape(-1, channels)

time: 519 us -> 544 us (1.048)
  local copies, waits for them, and re-layouts: 163 us -> 175 us
  waiting for transfers between devices: 56.7 us -> 65.3 us
  other arithmetic: 98.3 us -> 105 us
    unnamed x82 -> x85, local copies, waits for them, and re-layouts: 49.7 us -> 50.2 us
  transfers between devices with their start and end apart: 6 -> 8, of which waited for: 2 -> 3; matrix products, arithmetic and copies ran while one was open for 45% -> 46% of each run, Pallas kernels for 0% -> 0%
where the time goes in v1:
time: 544 us; the launch traced here: 536 us
  local copies, waits for them, and re-layouts  175 us (32%)
  matrix products  136 us (25%)
  other arithmetic  105 us (19%)
  waiting for transfers between devices  65.3 us (12%)
  blocking collectives  39.3 us (7%)
  between operations  15.6 us (3%)
    squeeze x2, local copies, waits for them, and re-layouts, conv_back(): moved = jnp.pad(pulled[:, :, :, :, tap_index], widths)  62.2 us
    unnamed x85, local copies, waits for them, and re-layouts  50.2 us
    psum x1, waiting for transfers between devices, per_device(): lax.psum(shards[0].astype(jnp.bfloat16), 'dp').astype(jnp.float32)  46.8 us
    dot_general x2, matrix products, conv_apply(): jnp.einsum('pc,tcd->ptd', flat_padded, taps_weight, preferred_element_typ...  45.9 us
    dot_general x2, matrix products, conv_back(): jnp.einsum('pd,tcd->ptc', flat_grad, taps_weight, preferred_element_type=...  36.3 us
    add x2, other arithmetic, conv_back(): spread = moved if spread is None else spread + moved  33.5 us
    dot_general x2, matrix products, conv_back(): jnp.einsum('pc,ptd->tcd', flat_padded, stacked, preferred_element_type=jn...  29.2 us
    psum x1, blocking collectives, per_device(): lax.psum(shards[2].astype(jnp.bfloat16), 'dp').astype(jnp.float32)  23.7 us
  transfers between devices with their start and end apart: 8, of which 3 were waited for; matrix products, arithmetic and copies ran while one was open for 46% of the time, Pallas kernels for 0%

profile of v1, /device:TPU:0, one launch (start us, length us, event | category | flops | bytes accessed | tf_op | source)
XLA Modules:
  0.0 536.0 jit_solution(16305828818428210135)
XLA Ops:
  7.9 5.0 fusion.79
  19.4 16.4 %reduce-scatter.10.cloned.1.call-done = bf16[64,256]{1,0:T(8,128)(2,1)} async-done(((bf16[256,256]{1,0:T(8,128)(2,1)}), bf16[64,256]{1,0:T(8,128)(2,1)}) %reduce-scatter.10.cloned.1.call-update) | async-done | bytes 32784 | tf_op jit(solution)/shard_map/reduce_scatter | solution.py:204
  35.8 23.7 %psum.23 = bf16[64,256]{1,0:T(8,128)(2,1)S(1)} all-reduce(bf16[64,256]{1,0:T(8,128)(2,1)} %reduce-scatter.10.cloned.1.call-done), channel_id=1, replica_groups=mesh['dp'=8,'fsdp'=4] {'dp'}, use_global_device_ids=true, to_apply=%region_5.6 | all-reduce | flops 16384 | bytes 65536 | tf_op jit(solution)/shard_map/psum | solution.py:213
  60.2 3.8 maximum_bitcast_fusion
  64.0 1.9 collective-permute-done
  66.1 2.2 fusion.35
  68.3 1.9 copy.310
  70.2 2.0 reshape_squeeze.3
  72.3 15.6 %all_gather.13 = bf16[256,256]{1,0:T(8,128)(2,1)} all-gather(bf16[64,256]{1,0:T(8,128)(2,1)S(1)} %get-tuple-element.194), channel_id=1, replica_groups=mesh['dp'=8,'fsdp'=4] {'fsdp'}, dimensions={0}, use_global_device_ids=true | all-gather | bytes 163840 | tf_op jit(solution)/shard_map/all_gather | solution.py:176
  88.0 2.2 convolution_bitcast_fusion
  90.1 2.9 copy.311
  93.1 4.8 reshape.705
  97.9 23.2 %fusion.33 = f32[8,12,8,8,9,256]{5,3,4,2,1,0:T(8,128)} fusion(bf16[9,256,256,1,1,1]{2,1,0,5,4,3:T(8,128)(2,1)} %bitcast.411, bf16[8,12,8,8,256,1]{4,1,3,0,2,5:T(8,128)(2,1)} %maximum_bitcast_fusion), kind=kOutput, calls=%fused_computation.103 | convolution fusion | flops 7247757312 | bytes 60948480 | tf_op jit(solution)/shard_map/pc,tcd->ptd/dot_general | solution.py:82
  121.1 17.8 %multiply_convert_fusion = (bf16[8,12,6,6,256]{4,3,2,1,0:T(8,128)(2,1)S(1)}, f32[8,12,6,6,256]{4,3,2,1,0:T(8,128)}) fusion(f32[8,12,8,8,9,256]{5,3,4,2,1,0:T(8,128)} %fusion.33), kind=kLoop, calls=%fused_computation.79 | loop fusion | flops 15040512 | bytes 37158912 | tf_op jit(solution)/shard_map/convert_element_type | solution.py:121
  145.2 22.7 %fusion.110 = f32[8,12,8,8,9,256]{5,3,2,1,0,4:T(8,128)} fusion(bf16[9,256,256,1,1,1]{2,1,5,4,3,0:T(8,128)(2,1)} %bitcast.409, bf16[8,12,1,8,256]{4,3,2,1,0:T(8,128)(2,1)} %copy.300, bf16[8,12,6,1,256]{4,3,2,1,0:T(2,128)(2,1)S(1)} %copy.295, bf16[8,12,6,6,256]{4,3,2,1,0:T(8,128)(2,1)S(1)} %get-tuple-element.164, bf16[8,12,6,1,256]{4,3,2,1,0:T(2,128)(2,1)S(1)} %copy.294, ...), kind=kOutput, calls=%fused_computation.208 | convolution fusion | flops 7263485952 | bytes 60948480 | tf_op jit(solution)/shard_map/pc,tcd->ptd/dot_general | solution.py:82
  167.9 18.1 %fusion.7 = (bf16[8,12,6,6,256]{4,3,2,1,0:T(8,128)(2,1)S(1)}, f32[8,12,6,6,1,256]{5,3,2,1,0,4:T(8,128)}) fusion(bf16[8]{0:T(256)(128)(2,1)S(1)} %copy-done.30, bf16[1,8,12,6,6,256]{5,1,4,3,2,0:T(8,128)(2,1)S(1)} %copy-done.1, f32[8,12,8,8,9,256]{5,3,2,1,0,4:T(8,128)} %fusion.110), kind=kLoop, calls=%fused_computation.20 | loop fusion | flops 26542080 | bytes 38928400 | tf_op jit(solution)/shard_map/convert_element_type | solution.py:187
  186.0 19.7 %fusion.36 = f32[8,12,6,6,9,256]{5,3,2,1,0,4:T(8,128)} fusion(bf16[9,256,256,1,1,1]{2,1,5,4,3,0:T(8,128)(2,1)S(1)} %bitcast.410, f32[8,12,6,6,1,256]{5,3,2,1,0,4:T(8,128)} %get-tuple-element.163, bf16[1,8,12,6,6,256]{5,1,4,3,2,0:T(8,128)(2,1)} %param.30, bf16[8]{0:T(256)(128)(2,1)} %copy-done.29), kind=kOutput, calls=%fused_computation.110 | convolution fusion | flops 4098097152 | bytes 38338576 | tf_op jit(solution)/shard_map/pd,tcd->ptc/dot_general | solution.py:97
  205.7 30.6 %slice_bitcast_fusion.17 = (f32[8,12,6,6,256]{4,3,2,1,0:T(8,128)}, f32[8,12,6,6,256]{4,3,2,1,0:T(8,128)}, f32[8,12,6,6,256]{4,3,2,1,0:T(8,128)}, f32[8,12,6,6,25...) fusion(f32[8,12,6,6,9,256]{5,3,2,1,0,4:T(8,128)} %fusion.36), kind=kLoop, calls=%fused_computation.57 | loop fusion | bytes 63700992 | tf_op jit(solution)/shard_map/squeeze | solution.py:103
  236.3 18.5 %pad_add_fusion.1 = f32[8,12,8,8,256]{4,3,2,1,0:T(8,128)} fusion(f32[8,12,6,6,256]{4,3,2,1,0:T(8,128)} %get-tuple-element.183, f32[8,12,6,6,256]{4,3,2,1,0:T(8,128)} %get-tuple-element.176, f32[8,12,6,6,256]{4,3,2,1,0:T(8,128)} %get-tuple-element.177, f32[8,12,6,6,256]{4,3,2,1,0:T(8,128)} %get-tuple-element.178, f32[8,12,6,6,256]{4,3,2,1,0:T(8,128)} %get-tuple-element.179, ...), kind=kLoop, calls=%fused_computation.7 | loop fusion | flops 12582912 | bytes 38141952 | tf_op jit(solution)/shard_map/add | solution.py:104
  254.8 4.9 fusion.171
  259.7 2.7 slice_bitcast_fusion.26
  262.4 5.3 slice.563
  267.7 2.3 bitcast_dynamic-update-slice_fusion.8
  270.0 2.5 bitcast_dynamic-update-slice_fusion.7
  272.4 2.5 bitcast_dynamic-update-slice_fusion.6
  274.9 2.4 bitcast_dynamic-update-slice_fusion.5
  277.3 2.4 bitcast_dynamic-update-slice_fusion.4
  279.7 2.4 bitcast_dynamic-update-slice_fusion.3
  282.1 2.4 bitcast_dynamic-update-slice_fusion.2
  284.5 2.5 bitcast_dynamic-update-slice_fusion.1
  287.0 2.4 bitcast_dynamic-update-slice_fusion
  289.4 13.9 %bitcast_convert_fusion = bf16[9,256,256]{1,2,0:T(8,128)(2,1)} fusion(bf16[8,12,8,8,9,256]{5,3,2,1,0,4:T(8,128)(2,1)} %bitcast_dynamic-update-slice_fusion, bf16[8,12,1,8,256]{4,3,2,1,0:T(8,128)(2,1)S(1)} %copy-done.20, bf16[8,12,6,1,256]{4,3,2,1,0:T(2,128)(2,1)S(1)} %copy-done.18, bf16[8,12,6,6,256]{4,3,2,1,0:T(8,128)(2,1)S(1)} %copy-done.3, ...), kind=kOutput, calls=%fused_computation.108 | convolution fusion | flops 7264075776 | bytes 32636928 | tf_op jit(solution)/shard_map/pc,ptd->tcd/dot_general | solution.py:108
  305.9 2.5 fusion.85
  308.4 3.2 slice_add_fusion.19
  311.7 13.4 %scatter-add.29 = f32[8,12,6,6,256]{4,3,2,1,0:T(8,128)} dynamic-update-slice(f32[8,12,6,6,256]{4,3,2,1,0:T(8,128)} %fusion.85, f32[8,12,6,1,256]{4,3,2,1,0:T(1,128)S(1)} %slice_add_fusion.19, s32[]{:T(128)} %constant.229.clone.1, s32[]{:T(128)} %constant.229.clone.1, s32[]{:T(128)} %constant.229.clone.1, s32[]{:T(128)} %constant.229.clone.1, s32[]{:T(128)} %constant.229.clone.1) | dynamic-update-slice | bytes 1179652 | tf_op jit(solution)/shard_map/scatter-add | solution.py:65
  325.0 2.5 fusion.84
  327.5 3.4 slice_add_fusion.18
  330.9 13.0 %scatter-add.31 = f32[8,12,6,6,256]{4,3,2,1,0:T(8,128)} dynamic-update-slice(f32[8,12,6,6,256]{4,3,2,1,0:T(8,128)} %fusion.84, f32[8,12,6,1,256]{4,3,2,1,0:T(1,128)S(1)} %slice_add_fusion.18, s32[]{:T(128)} %constant.229.clone.1, s32[]{:T(128)} %constant.229.clone.1, s32[]{:T(128)} %constant.229.clone.1, s32[]{:T(128)} %constant.233.clone.1, s32[]{:T(128)} %constant.229.clone.1) | dynamic-update-slice | bytes 1179652 | tf_op jit(solution)/shard_map/scatter-add | solution.py:71
  343.9 5.5 %fusion.16 = bf16[8,12,6,6,256]{4,3,2,1,0:T(8,128)(2,1)S(1)} fusion(f32[8,12,6,6,256]{4,3,2,1,0:T(8,128)} %get-tuple-element.165, f32[8,12,6,6,256]{4,3,2,1,0:T(8,128)} %scatter-add.31), kind=kLoop, calls=%fused_computation.29 | loop fusion | flops 17694720 | bytes 8847360 | tf_op jit(solution)/shard_map/convert_element_type | solution.py:191
  349.4 2.3 bitcast_dynamic-update-slice_fusion.17
  351.7 2.4 bitcast_dynamic-update-slice_fusion.16
  354.2 2.4 bitcast_dynamic-update-slice_fusion.15
  356.6 2.3 bitcast_dynamic-update-slice_fusion.14
  358.9 2.5 bitcast_dynamic-update-slice_fusion.13
  361.3 2.5 bitcast_dynamic-update-slice_fusion.12
  363.8 2.4 bitcast_dynamic-update-slice_fusion.11
  366.2 2.4 bitcast_dynamic-update-slice_fusion.10
  368.6 2.5 bitcast_dynamic-update-slice_fusion.9
  371.1 16.7 %fusion.41 = f32[8,12,6,6,9,256]{5,1,4,3,2,0:T(8,128)} fusion(bf16[9,256,256,1,1,1]{2,1,0,5,4,3:T(8,128)(2,1)S(1)} %bitcast.412, bf16[8,12,6,6,256,1]{4,3,2,1,0,5:T(8,128)(2,1)S(1)} %bitcast.403), kind=kOutput, calls=%fused_computation.115 | convolution fusion | flops 4076863488 | bytes 34799616 | tf_op jit(solution)/shard_map/pd,tcd->ptc/dot_general | solution.py:97
  387.7 31.6 %slice_bitcast_fusion.8 = (f32[8,12,6,6,256]{4,1,3,2,0:T(8,128)}, f32[8,12,6,6,256]{4,1,3,2,0:T(8,128)}, f32[8,12,6,6,256]{4,1,3,2,0:T(8,128)}, f32[8,12,6,6,256...) fusion(f32[8,12,6,6,9,256]{5,1,4,3,2,0:T(8,128)} %fusion.41), kind=kLoop, calls=%fused_computation.48 | loop fusion | bytes 63700992 | tf_op jit(solution)/shard_map/squeeze | solution.py:103
  419.3 15.3 %bitcast_convert_fusion.1 = bf16[9,256,256]{1,2,0:T(8,128)(2,1)} fusion(bf16[8,12,8,8,9,256]{5,3,2,1,0,4:T(8,128)(2,1)} %bitcast_dynamic-update-slice_fusion.9, bf16[8,12,8,8,256,1]{4,1,3,0,2,5:T(8,128)(2,1)} %maximum_bitcast_fusion), kind=kOutput, calls=%fused_computation.109 | convolution fusion | flops 7248347136 | bytes 32636928 | tf_op jit(solution)/shard_map/pc,ptd->tcd/dot_general | solution.py:108
  434.7 5.4 %fusion.29 = bf16[1,8,12,6,6,256]{5,4,3,2,1,0:T(8,128)(2,1)S(1)} fusion(f32[1,8,12,6,6,256]{5,4,3,2,1,0:T(8,128)} %reshape.705, f32[8,12,6,6,1,256]{5,3,2,1,0,4:T(8,128)} %get-tuple-element.163), kind=kLoop, calls=%fused_computation.77 | loop fusion | flops 8847360 | bytes 8847360 | tf_op jit(solution)/shard_map/convert_element_type | solution.py:172
  440.0 3.1 copy.351
  443.1 15.0 %pad_add_fusion = f32[8,12,8,8,256]{4,1,3,2,0:T(8,128)S(1)} fusion(f32[8,12,6,6,256]{4,1,3,2,0:T(8,128)} %get-tuple-element.173, f32[8,12,6,6,256]{4,1,3,2,0:T(8,128)} %get-tuple-element.174, f32[8,12,6,6,256]{4,1,3,2,0:T(8,128)} %get-tuple-element.167, f32[8,12,6,6,256]{4,1,3,2,0:T(8,128)} %get-tuple-element.168, f32[8,12,6,6,256]{4,1,3,2,0:T(8,128)} %get-tuple-element.169, ...), kind=kLoop, calls=%fused_computation | loop fusion | flops 12582912 | bytes 38141952 | tf_op jit(solution)/shard_map/add | solution.py:104
  458.2 2.7 slice.581
  460.9 1.4 fusion.56
  462.3 2.6 fusion.58
  464.9 2.5 fusion.60
  467.4 2.5 fusion.62
  470.0 3.3 add_bitcast_fusion
  473.4 3.8 copy.352
  477.2 46.8 %all-reduce.43.cloned.1.call-done = (bf16[576,256]{1,0:T(8,128)(2,1)}, bf16[576,256]{1,0:T(8,128)(2,1)}) async-done(((bf16[576,256]{1,0:T(8,128)(2,1)}, bf16[576,256]{1,0:T(8,128)(2,1)}), (bf16[576,256]{1,0:T(8,128)(2,1)}, bf16[576,256]{1,0:T(8,128)(2,1)})) %all-reduce.43.cloned.1.call-update) | async-done | bytes 589840 | tf_op jit(solution)/shard_map/psum | solution.py:211
  524.0 2.4 multiply_subtract_fusion.1
  526.5 2.4 multiply_subtract_fusion
  (122 shorter events, 16.0 us)
Async XLA Ops:
  7.2 28.6 %reduce-scatter.10.cloned.1.call-start = ((), (), s32[]{:S(2)}) async-start(), calls=%async_computation.7 | async-start | bytes 163840 | tf_op jit(solution)/shard_map/reduce_scatter | solution.py:204
  7.9 58.2 %copy-start.29 = (bf16[8]{0:T(256)(128)(2,1)}, bf16[8]{0:T(256)(128)(2,1)S(1)}, u32[]{:S(2)}) copy-start(bf16[8]{0:T(256)(128)(2,1)S(1)} %compare_convert_fusion) | copy-start | bytes 52
  7.9 5.9 %copy-start.11 = (f32[576,256]{1,0:T(8,128)S(1)}, f32[576,256]{1,0:T(8,128)}, u32[]{:S(2)}) copy-start(f32[576,256]{1,0:T(8,128)} %param.33) | copy-start | bytes 1769476
  7.9 6.7 %copy-start.13 = (f32[576,256]{1,0:T(8,128)S(1)}, f32[576,256]{1,0:T(8,128)}, u32[]{:S(2)}) copy-start(f32[576,256]{1,0:T(8,128)} %param.34) | copy-start | bytes 1769476
  7.9 7.6 %copy-start.6 = (bf16[1,8,12,6,6,256]{5,1,4,3,2,0:T(8,128)(2,1)S(1)}, bf16[1,8,12,6,6,256]{5,1,4,3,2,0:T(8,128)(2,1)}, u32[]{:S(2)}) copy-start(bf16[1,8,12,6,6,256]{5,1,4,3,2,0:T(8,128)(2,1)} %param.29) | copy-start | bytes 5308420
  13.0 3.6 copy-start.31
  13.8 84.2 %all-gather.3.cloned.1.call-start = ((), (), s32[]{:S(2)}) async-start(), calls=%async_computation.3 | async-start | bytes 1474560 | tf_op jit(solution)/shard_map/all_gather | solution.py:163
  14.6 129.8 %all-gather.5.cloned.1.call-start = ((), (), s32[]{:S(2)}) async-start(), calls=%async_computation.4 | async-start | bytes 1474560 | tf_op jit(solution)/shard_map/all_gather | solution.py:164
  15.4 454.6 %reduce-scatter.8.cloned.1.call-start = ((), (), s32[]{:S(2)}) async-start(), calls=%async_computation.6 | async-start | bytes 1474560 | tf_op jit(solution)/shard_map/reduce_scatter | solution.py:201
  16.6 2.7 copy-start.4
  16.6 42.9 %copy-start.26 = (f32[64,256]{1,0:T(8,128)S(1)}, f32[64,256]{1,0:T(8,128)}, u32[]{:S(2)}) copy-start(f32[64,256]{1,0:T(8,128)} %param.35) | copy-start | bytes 196612
  16.6 42.9 %copy-start.27 = (f32[64,256]{1,0:T(8,128)S(1)}, f32[64,256]{1,0:T(8,128)}, u32[]{:S(2)}) copy-start(f32[64,256]{1,0:T(8,128)} %param.40) | copy-start | bytes 196612
  16.6 42.9 %copy-start.28 = (f32[64,256]{1,0:T(8,128)S(1)}, f32[64,256]{1,0:T(8,128)}, u32[]{:S(2)}) copy-start(f32[64,256]{1,0:T(8,128)} %param.41) | copy-start | bytes 196612
  19.4 46.7 %copy-start = (bf16[1,8,12,6,6,256]{5,1,4,3,2,0:T(8,128)(2,1)S(1)}, bf16[1,8,12,6,6,256]{5,1,4,3,2,0:T(8,128)(2,1)}, u32[]{:S(2)}) copy-start(bf16[1,8,12,6,6,256]{5,1,4,3,2,0:T(8,128)(2,1)} %param.30) | copy-start | bytes 5308420
  60.2 5.8 %collective-permute-start = (bf16[1,64,256]{2,1,0:T(8,128)(2,1)S(1)}, bf16[1,64,256]{2,1,0:T(8,128)(2,1)S(1)}, u32[]{:S(2)}, u32[]{:S(2)}) collective-permute-start(bf16[1,64,256]{2,1,0:T(8,128)(2,1)S(1)} %bitcast.420), channel_id=1, source_target_pairs={{0,1},{1,0},{2,3},{3,2},{4,5},{5,4},{6,7},{7,6},{8,9},{9,8},{10,11... | collective-permute-start | bytes 98312 | tf_op jit(solution)/shard_map/ppermute | solution.py:22
  66.0 21.9 %collective-permute-start.1 = (bf16[2,64,256]{2,1,0:T(8,128)(2,1)S(1)}, bf16[2,64,256]{2,1,0:T(8,128)(2,1)S(1)}, u32[]{:S(2)}, u32[]{:S(2)}) collective-permute-start(bf16[2,64,256]{2,1,0:T(8,128)(2,1)S(1)} %get-tuple-element.196), channel_id=1, source_target_pairs={{0,2},{1,3},{2,0},{3,1},{4,6},{5,7},{6,4},{7,5},{8,10},{9,11},{10,... | collective-permute-start | bytes 196616 | tf_op jit(solution)/shard_map/ppermute | solution.py:22
  138.9 5.5 %copy-start.2 = (bf16[8,12,6,6,256]{4,3,2,1,0:T(8,128)(2,1)}, bf16[8,12,6,6,256]{4,3,2,1,0:T(8,128)(2,1)S(1)}, u32[]{:S(2)}) copy-start(bf16[8,12,6,6,256]{4,3,2,1,0:T(8,128)(2,1)S(1)} %get-tuple-element.164) | copy-start | bytes 5308420
  143.6 0.9 copy-start.15
  144.4 0.8 copy-start.17
  145.2 22.7 %copy-start.1 = (bf16[1,8,12,6,6,256]{5,1,4,3,2,0:T(8,128)(2,1)S(1)}, bf16[1,8,12,6,6,256]{5,1,4,3,2,0:T(8,128)(2,1)}, u32[]{:S(2)}) copy-start(bf16[1,8,12,6,6,256]{5,1,4,3,2,0:T(8,128)(2,1)} %param.30) | copy-start | bytes 5308420
  145.2 22.7 %copy-start.30 = (bf16[8]{0:T(256)(128)(2,1)S(1)}, bf16[8]{0:T(256)(128)(2,1)}, u32[]{:S(2)}) copy-start(bf16[8]{0:T(256)(128)(2,1)} %copy-done.29) | copy-start | bytes 52
  167.9 18.1 %copy-start.7 = (bf16[2304,256]{1,0:T(8,128)(2,1)S(1)}, bf16[2304,256]{1,0:T(8,128)(2,1)}, u32[]{:S(2)}) copy-start(bf16[2304,256]{1,0:T(8,128)(2,1)} %all-gather.5.cloned.1.call-done) | copy-start | bytes 3538948
  284.5 4.9 copy-start.3
  284.5 4.9 copy-start.16
  284.5 4.9 copy-start.18
  284.5 4.9 copy-start.19
  284.5 4.9 copy-start.20
  303.3 1.1 copy-start.10
  303.3 1.8 copy-start.9
  303.4 166.6 %reduce-scatter.6.cloned.1.call-start = ((), (), s32[]{:S(2)}) async-start(), calls=%async_computation.5 | async-start | bytes 1474560 | tf_op jit(solution)/shard_map/reduce_scatter | solution.py:198
  366.2 4.9 copy-start.8
  434.6 89.4 %all-reduce.43.cloned.1.call-start = ((), (), s32[]{:S(2)}) async-start(), calls=%async_computation.8 | async-start | bytes 1179648 | tf_op jit(solution)/shard_map/psum | solution.py:211
  460.9 9.1 %copy-start.5 = (bf16[8,12,6,6,256]{4,3,2,1,0:T(8,128)(2,1)S(1)}, bf16[8,12,6,6,256]{4,3,2,1,0:T(8,128)(2,1)}, u32[]{:S(2)}) copy-start(bf16[8,12,6,6,256]{4,3,2,1,0:T(8,128)(2,1)} %fusion.35) | copy-start | bytes 5308420
  460.9 9.1 %copy-start.25 = (bf16[256,256]{1,0:T(8,128)(2,1)S(1)}, bf16[256,256]{1,0:T(8,128)(2,1)}, u32[]{:S(2)}) copy-start(bf16[256,256]{1,0:T(8,128)(2,1)} %all_gather.13) | copy-start | bytes 393220
  473.3 50.8 %copy-start.12 = (f32[576,256]{1,0:T(8,128)S(1)}, f32[576,256]{1,0:T(8,128)}, u32[]{:S(2)}) copy-start(f32[576,256]{1,0:T(8,128)} %param.33) | copy-start | bytes 1769476
  473.3 50.7 %copy-start.21 = (f32[576,256]{1,0:T(8,128)S(1)}, f32[576,256]{1,0:T(8,128)}, u32[]{:S(2)}) copy-start(f32[576,256]{1,0:T(8,128)} %param.36) | copy-start | bytes 1769476
  473.3 50.7 %copy-start.22 = (f32[576,256]{1,0:T(8,128)S(1)}, f32[576,256]{1,0:T(8,128)}, u32[]{:S(2)}) copy-start(f32[576,256]{1,0:T(8,128)} %param.37) | copy-start | bytes 1769476
  473.3 53.2 %copy-start.14 = (f32[576,256]{1,0:T(8,128)S(1)}, f32[576,256]{1,0:T(8,128)}, u32[]{:S(2)}) copy-start(f32[576,256]{1,0:T(8,128)} %param.34) | copy-start | bytes 1769476
  473.3 53.2 %copy-start.23 = (f32[576,256]{1,0:T(8,128)S(1)}, f32[576,256]{1,0:T(8,128)}, u32[]{:S(2)}) copy-start(f32[576,256]{1,0:T(8,128)} %param.38) | copy-start | bytes 1769476
  473.4 53.1 %copy-start.24 = (f32[576,256]{1,0:T(8,128)S(1)}, f32[576,256]{1,0:T(8,128)}, u32[]{:S(2)}) copy-start(f32[576,256]{1,0:T(8,128)} %param.39) | copy-start | bytes 1769476
Sparse Core Ops, SparseCore 0:
  13.9 21.8 reduce-scatter.9
  38.0 28.9 all-gather.2
  69.3 31.9 all-gather.4
  303.5 27.7 reduce-scatter.7
  434.7 28.0 reduce-scatter.5
  470.1 53.8 all-reduce.42
